TPU v7x, 128 devices: a whole 4x4x4 slice. The times are simulated.
128 devices in a mesh: row: 8 (over y_lo, z), col: 16 (over x, y_hi, core).
Axes of the slice: x: 4, y: 4 (y_hi: 2, y_lo: 2; y = y_hi * 2 + y_lo), z: 4, core: 2. Of those that a mesh axis runs over, the one named last changes fastest.
Arguments:
- feats_one: bfloat16 [65536, 256], P(('row', 'col')), may hold values from -6 to 6
- feats_two: bfloat16 [65536, 256], P(('row', 'col')), may hold values from -6 to 6
- target_view: bfloat16 [65536, 256], P(('row', 'col')), may hold values from -6 to 6
- negatives: int32 [65536], P(('row', 'col')), may hold values from 0 to 511
- weight_one: bfloat16 [256, 256], replicated, may hold values from -0.375 to 0.375
- weight_two: bfloat16 [256, 256], replicated, may hold values from -0.375 to 0.375
- block_tiles: bfloat16 [81920, 128, 128], P(('row', 'col')), may hold values from -0.15625 to 0.15625
- tile_rows: int32 [81920], P(('row', 'col')), may hold values from 0 to 31
- tile_cols: int32 [81920], P(('row', 'col')), may hold values from 0 to 31
- block_counts: int32 [128], P(('row', 'col')), may hold values from 80 to 640, as said below
- need_rows: int32 [128, 16, 2], P(('row', 'col')), may hold values from 0 to 3, as said below
Outputs:
- grad_hidden: bfloat16 [65536, 256], P(('row', 'col'))
- grad_first: float32 [256, 256], replicated
- grad_second: float32 [256, 256], replicated
Inputs may be any that keep to these rules, and one draw needn't show every extreme that they name: `need_rows`: for each owner and source, the 2 entries are distinct. `block_counts`: live tiles of one block list.
All inputs are finite; a program needn't handle non-finite values.
Results may differ from a plain program's by a relative error of at most 0.0063.
Values may be sent and summed in bfloat16 or wider, within the bound.
No kernel may reach another device: no remote copies, remote signals or barrier semaphores. Data moves between devices by JAX's collectives and lax.ppermute only.
A program may use at most 192 MiB of HBM per device.

v0:
```python
import math
import jax
import jax.numpy as jnp
from jax import lax
from jax.sharding import PartitionSpec as P


def silu_slope(values):
    sig = jax.nn.sigmoid(values)
    return sig * (1.0 + values * (1.0 - sig))


def column_product(left, right):
    return lax.dot_general(
        left, right, (((0,), (0,)), ((), ())), preferred_element_type=jnp.float32
    )


def on_device(
    feats_one,
    feats_two,
    target_view,
    negatives,
    weight_one,
    weight_two,
    block_tiles,
    tile_rows,
    tile_cols,
    block_counts,
    need_rows,
):
    node_dev, features = feats_two.shape
    capacity, tile_size = (block_tiles.shape[0], block_tiles.shape[1])
    sources = lax.axis_size("col")
    row_group = lax.axis_size("row")
    tiles_dev = node_dev // tile_size
    slot_count = need_rows.shape[2]
    col_count = row_group * tiles_dev
    inverse_root = 1.0 / math.sqrt(features)
    weight_norm = 1.0 / math.sqrt(node_dev * row_group * sources)
    pre_two = jnp.dot(feats_two, weight_two, preferred_element_type=jnp.float32)
    hidden = jax.nn.silu(pre_two)
    partner_rows = hidden[negatives]
    target_full = target_view.astype(jnp.float32)
    s_pos = jnp.sum(hidden * target_full, axis=-1) * inverse_root
    s_neg = jnp.sum(hidden * partner_rows, axis=-1) * inverse_root
    prob_pos = jax.nn.sigmoid(-s_pos)
    prob_neg = jax.nn.sigmoid(s_neg)
    grad_out = -prob_pos[:, None] * target_full + prob_neg[:, None] * partner_rows
    grad_out = grad_out + jax.ops.segment_sum(
        prob_neg[:, None] * hidden, negatives, num_segments=node_dev
    )
    dpre_two = (grad_out * silu_slope(pre_two)).astype(jnp.bfloat16)
    grad_second = column_product(feats_two, dpre_two)
    grad_second = lax.psum(grad_second, ("row", "col"))
    message = lax.dot_general(
        dpre_two, weight_two, (((1,), (1,)), ((), ())), preferred_element_type=jnp.float32
    ).astype(jnp.bfloat16)
    gathered = lax.all_gather(message, "col", axis=0, tiled=True)
    buffer_tiles = gathered.reshape(sources * tiles_dev, tile_size, features)
    need_flat = need_rows[0].reshape(-1)
    slot_ids = jnp.arange(sources * slot_count, dtype=jnp.int32)
    local_tile = jnp.sum(
        jnp.where(tile_rows[:, None] == slot_ids[None, :], need_flat[None, :], 0), axis=1
    )
    row_tile = tile_rows // slot_count * tiles_dev + local_tile
    block_len = 128
    rounds = capacity // block_len
    live = (jnp.arange(capacity, dtype=jnp.int32) < block_counts[0]).astype(jnp.float32)
    column_ids = jnp.arange(col_count, dtype=jnp.int32)

    def add_block(summed_tiles, pieces):
        tile_part, row_part, col_part, live_part = pieces
        gathered_rows = buffer_tiles[row_part]
        contrib = jnp.einsum(
            "ktu,ktf->kuf", tile_part, gathered_rows, preferred_element_type=jnp.float32
        )
        selector = jnp.where(col_part[:, None] == column_ids[None, :], live_part[:, None], 0.0)
        placed = jnp.einsum(
            "kc,kuf->cuf",
            selector,
            contrib,
            precision=lax.Precision.HIGHEST,
            preferred_element_type=jnp.float32,
        )
        return (summed_tiles + placed, None)

    start_tiles = jnp.zeros((col_count, tile_size, features), jnp.float32)
    summed_tiles, _ = lax.scan(
        add_block,
        start_tiles,
        (
            block_tiles.reshape(rounds, block_len, tile_size, tile_size),
            row_tile.reshape(rounds, block_len),
            tile_cols.reshape(rounds, block_len),
            live.reshape(rounds, block_len),
        ),
    )
    column_total = lax.psum_scatter(
        summed_tiles.reshape(col_count * tile_size, features),
        "row",
        scatter_dimension=0,
        tiled=True,
    )
    grad_hidden = column_total.astype(jnp.bfloat16)
    pre_one = jnp.dot(feats_one, weight_one, preferred_element_type=jnp.float32)
    dpre_one = (grad_hidden.astype(jnp.float32) * silu_slope(pre_one)).astype(jnp.bfloat16)
    grad_first = column_product(feats_one, dpre_one)
    grad_first = lax.psum(grad_first, ("row", "col"))
    return (grad_hidden, grad_first * weight_norm, grad_second * weight_norm)


def solution(mesh):
    return jax.shard_map(
        on_device,
        mesh=mesh,
        in_specs=(
            P(("row", "col"), None),
            P(("row", "col"), None),
            P(("row", "col"), None),
            P(("row", "col")),
            P(),
            P(),
            P(("row", "col"), None, None),
            P(("row", "col")),
            P(("row", "col")),
            P(("row", "col")),
            P(("row", "col"), None, None),
        ),
        out_specs=(P(("row", "col"), None), P(), P()),
        check_vma=False,
    )
```

profile of v0, /device:TPU:1, one launch (start us, length us, event | category | flops | bytes accessed | tf_op | source)
XLA Modules:
  0.0 544.5 jit_solution(12721467284938459450)
XLA Ops:
  7.2 1.0 copy-done
  8.2 1.2 fusion.22
  10.4 1.6 gather_fusion.1
  13.1 3.5 scatter_fusion
  17.0 1.0 convolution_convert_fusion
  18.1 27.9 %copy.40 = bf16[640,128,128]{1,2,0:T(8,128)(2,1)} copy(bf16[640,128,128]{2,1,0:T(8,128)(2,1)} %param.19) | data formatting | bytes 41943040 | tf_op args[6]
  47.0 30.8 %all-gather.2.cloned.1.call-done = bf16[8192,256]{1,0:T(8,128)(2,1)} async-done(((bf16[512,256]{1,0:T(8,128)(2,1)}), bf16[8192,256]{1,0:T(8,128)(2,1)}) %all-gather.2.cloned.1.call-update) | async-done | bytes 4194320 | tf_op jit(solution)/shard_map/all_gather | solution.py:59
  77.8 241.0 %while.11 = (s32[]{:T(128)}, f32[32,128,256]{2,0,1:T(8,128)}, s32[5,128]{1,0:T(8,128)}, f32[5,128]{1,0:T(8,128)S(1)}, bf16[5,128,128,128]{2,3,1,0:T(8,128)(2,1)}...) while((s32[]{:T(128)}, f32[32,128,256]{2,0,1:T(8,128)}, ...), condition=%wide.region_5.6_spmd.clone, body=%wide.region_4.5_spmd.clone.sunk | while | flops 2686461440 | bytes 71313008 | solution.py:89
  77.8 8.7 %gather_fusion = bf16[128,128,256]{2,1,0:T(8,128)(2,1)} fusion(bf16[64,128,256]{2,1,0:T(8,128)(2,1)} %get-tuple-element.172, s32[1024]{0:T(1024)S(1)} %pad_clamp_fusion.3), kind=kCustom, calls=%fused_computation.clone.clone.1 | custom fusion | bytes 16777728 | tf_op jit(solution)/shard_map/while/body/eval_jaxpr/gather | solution.py:74
  86.5 12.8 %fusion.55 = f32[128,128,256]{2,1,0:T(8,128)} fusion(bf16[128,128,256]{2,1,0:T(8,128)(2,1)} %gather_fusion, bf16[5,128,128,128]{2,3,1,0:T(8,128)(2,1)} %get-tuple-element.170, s32[]{:T(128)} %get-tuple-element.157), kind=kOutput, calls=%fused_computation.6.clone.1 | convolution fusion | flops 1073741824 | bytes 29360640 | tf_op jit(solution)/shard_map/while/body/eval_jaxpr/ktu,ktf->kuf/dot_general | solution.py:75
  100.0 25.4 %select_add_fusion.2 = f32[32,128,256]{2,0,1:T(8,128)} fusion(f32[32,128,256]{2,0,1:T(8,128)} %get-tuple-element.158, pred[]{:T(512)S(6)} %compare.5, f32[128,128,256]{2,1,0:T(8,128)} %fusion.55, f32[128]{0:T(128)S(1)} %fusion.56, s32[128]{0:T(128)S(1)} %fusion.57), kind=kOutput, calls=%fused_computation.8.clone.1 | convolution fusion | flops 1612718080 | bytes 25166848 | tf_op jit(solution)/shard_map/while/body/eval_jaxpr/kc,kuf->cuf/dot_general | solution.py:79
  125.5 8.7 %gather_fusion = bf16[128,128,256]{2,1,0:T(8,128)(2,1)} fusion(bf16[64,128,256]{2,1,0:T(8,128)(2,1)} %get-tuple-element.172, s32[1024]{0:T(1024)S(1)} %pad_clamp_fusion.3), kind=kCustom, calls=%fused_computation.clone.clone.1 | custom fusion | bytes 16777728 | tf_op jit(solution)/shard_map/while/body/eval_jaxpr/gather | solution.py:74
  134.2 12.8 %fusion.55 = f32[128,128,256]{2,1,0:T(8,128)} fusion(bf16[128,128,256]{2,1,0:T(8,128)(2,1)} %gather_fusion, bf16[5,128,128,128]{2,3,1,0:T(8,128)(2,1)} %get-tuple-element.170, s32[]{:T(128)} %get-tuple-element.157), kind=kOutput, calls=%fused_computation.6.clone.1 | convolution fusion | flops 1073741824 | bytes 29360640 | tf_op jit(solution)/shard_map/while/body/eval_jaxpr/ktu,ktf->kuf/dot_general | solution.py:75
  147.8 26.0 %select_add_fusion.2 = f32[32,128,256]{2,0,1:T(8,128)} fusion(f32[32,128,256]{2,0,1:T(8,128)} %get-tuple-element.158, pred[]{:T(512)S(6)} %compare.5, f32[128,128,256]{2,1,0:T(8,128)} %fusion.55, f32[128]{0:T(128)S(1)} %fusion.56, s32[128]{0:T(128)S(1)} %fusion.57), kind=kOutput, calls=%fused_computation.8.clone.1 | convolution fusion | flops 1612718080 | bytes 25166848 | tf_op jit(solution)/shard_map/while/body/eval_jaxpr/kc,kuf->cuf/dot_general | solution.py:79
  173.8 8.7 %gather_fusion = bf16[128,128,256]{2,1,0:T(8,128)(2,1)} fusion(bf16[64,128,256]{2,1,0:T(8,128)(2,1)} %get-tuple-element.172, s32[1024]{0:T(1024)S(1)} %pad_clamp_fusion.3), kind=kCustom, calls=%fused_computation.clone.clone.1 | custom fusion | bytes 16777728 | tf_op jit(solution)/shard_map/while/body/eval_jaxpr/gather | solution.py:74
  182.6 12.8 %fusion.55 = f32[128,128,256]{2,1,0:T(8,128)} fusion(bf16[128,128,256]{2,1,0:T(8,128)(2,1)} %gather_fusion, bf16[5,128,128,128]{2,3,1,0:T(8,128)(2,1)} %get-tuple-element.170, s32[]{:T(128)} %get-tuple-element.157), kind=kOutput, calls=%fused_computation.6.clone.1 | convolution fusion | flops 1073741824 | bytes 29360640 | tf_op jit(solution)/shard_map/while/body/eval_jaxpr/ktu,ktf->kuf/dot_general | solution.py:75
  196.1 26.0 %select_add_fusion.2 = f32[32,128,256]{2,0,1:T(8,128)} fusion(f32[32,128,256]{2,0,1:T(8,128)} %get-tuple-element.158, pred[]{:T(512)S(6)} %compare.5, f32[128,128,256]{2,1,0:T(8,128)} %fusion.55, f32[128]{0:T(128)S(1)} %fusion.56, s32[128]{0:T(128)S(1)} %fusion.57), kind=kOutput, calls=%fused_computation.8.clone.1 | convolution fusion | flops 1612718080 | bytes 25166848 | tf_op jit(solution)/shard_map/while/body/eval_jaxpr/kc,kuf->cuf/dot_general | solution.py:79
  222.2 8.8 %gather_fusion = bf16[128,128,256]{2,1,0:T(8,128)(2,1)} fusion(bf16[64,128,256]{2,1,0:T(8,128)(2,1)} %get-tuple-element.172, s32[1024]{0:T(1024)S(1)} %pad_clamp_fusion.3), kind=kCustom, calls=%fused_computation.clone.clone.1 | custom fusion | bytes 16777728 | tf_op jit(solution)/shard_map/while/body/eval_jaxpr/gather | solution.py:74
  230.9 12.8 %fusion.55 = f32[128,128,256]{2,1,0:T(8,128)} fusion(bf16[128,128,256]{2,1,0:T(8,128)(2,1)} %gather_fusion, bf16[5,128,128,128]{2,3,1,0:T(8,128)(2,1)} %get-tuple-element.170, s32[]{:T(128)} %get-tuple-element.157), kind=kOutput, calls=%fused_computation.6.clone.1 | convolution fusion | flops 1073741824 | bytes 29360640 | tf_op jit(solution)/shard_map/while/body/eval_jaxpr/ktu,ktf->kuf/dot_general | solution.py:75
  244.4 26.0 %select_add_fusion.2 = f32[32,128,256]{2,0,1:T(8,128)} fusion(f32[32,128,256]{2,0,1:T(8,128)} %get-tuple-element.158, pred[]{:T(512)S(6)} %compare.5, f32[128,128,256]{2,1,0:T(8,128)} %fusion.55, f32[128]{0:T(128)S(1)} %fusion.56, s32[128]{0:T(128)S(1)} %fusion.57), kind=kOutput, calls=%fused_computation.8.clone.1 | convolution fusion | flops 1612718080 | bytes 25166848 | tf_op jit(solution)/shard_map/while/body/eval_jaxpr/kc,kuf->cuf/dot_general | solution.py:79
  270.5 8.7 %gather_fusion = bf16[128,128,256]{2,1,0:T(8,128)(2,1)} fusion(bf16[64,128,256]{2,1,0:T(8,128)(2,1)} %get-tuple-element.172, s32[1024]{0:T(1024)S(1)} %pad_clamp_fusion.3), kind=kCustom, calls=%fused_computation.clone.clone.1 | custom fusion | bytes 16777728 | tf_op jit(solution)/shard_map/while/body/eval_jaxpr/gather | solution.py:74
  279.2 12.8 %fusion.55 = f32[128,128,256]{2,1,0:T(8,128)} fusion(bf16[128,128,256]{2,1,0:T(8,128)(2,1)} %gather_fusion, bf16[5,128,128,128]{2,3,1,0:T(8,128)(2,1)} %get-tuple-element.170, s32[]{:T(128)} %get-tuple-element.157), kind=kOutput, calls=%fused_computation.6.clone.1 | convolution fusion | flops 1073741824 | bytes 29360640 | tf_op jit(solution)/shard_map/while/body/eval_jaxpr/ktu,ktf->kuf/dot_general | solution.py:75
  292.8 26.0 %select_add_fusion.2 = f32[32,128,256]{2,0,1:T(8,128)} fusion(f32[32,128,256]{2,0,1:T(8,128)} %get-tuple-element.158, pred[]{:T(512)S(6)} %compare.5, f32[128,128,256]{2,1,0:T(8,128)} %fusion.55, f32[128]{0:T(128)S(1)} %fusion.56, s32[128]{0:T(128)S(1)} %fusion.57), kind=kOutput, calls=%fused_computation.8.clone.1 | convolution fusion | flops 1612718080 | bytes 25166848 | tf_op jit(solution)/shard_map/while/body/eval_jaxpr/kc,kuf->cuf/dot_general | solution.py:79
  318.8 5.9 %copy.49 = f32[32,128,256]{1,0,2:T(8,128)} copy(f32[32,128,256]{2,0,1:T(8,128)} %get-tuple-element.45) | data formatting | bytes 8388608 | tf_op jit(solution)/shard_map/while | solution.py:89
  324.8 8.0 %copy.62 = f32[32,8,32,128]{3,1,2,0:T(8,128)} copy(f32[32,8,32,128]{3,2,1,0:T(8,128)} %bitcast.62) | data formatting | bytes 8388608
  332.8 0.9 convolution_bitcast_fusion
  333.8 50.9 %reduce-scatter.2.cloned.1.call-done = f32[512,256]{0,1:T(8,128)} async-done(((f32[4096,256]{0,1:T(8,128)}), f32[512,256]{0,1:T(8,128)}) %reduce-scatter.2.cloned.1.call-update) | async-done | bytes 524304 | tf_op jit(solution)/shard_map/reduce_scatter | solution.py:99
  384.7 1.1 convert_element_type.26
  385.8 1.2 convolution_bitcast_fusion.1
  387.9 146.5 %all-reduce.3.cloned.1.call-done = (f32[256,256]{0,1:T(8,128)}, f32[256,256]{0,1:T(8,128)}) async-done(((f32[256,256]{0,1:T(8,128)}, f32[256,256]{0,1:T(8,128)}), (f32[256,256]{0,1:T(8,128)}, f32[256,256]{0,1:T(8,128)})) %all-reduce.3.cloned.1.call-update) | async-done | bytes 524304 | tf_op jit(solution)/shard_map/psum | solution.py:109
  534.4 1.0 broadcast_multiply_fusion.2
  536.2 1.0 broadcast_multiply_fusion.1
  (62 shorter events, 8.9 us)
Async XLA Ops:
  7.2 1.0 copy-start
  7.2 5.9 %copy-start.4 = (s32[512]{0:T(512)S(1)}, s32[512]{0:T(512)}, u32[]{:S(2)}) copy-start(s32[512]{0:T(512)} %param.16) | copy-start | bytes 6148
  7.2 4.9 copy-start.1
  7.2 70.6 %all-gather.2.cloned.1.call-start = ((), (), s32[]{:S(2)}) async-start(), calls=%async_computation.1 | async-start | bytes 4456448 | tf_op jit(solution)/shard_map/all_gather | solution.py:59
  12.3 4.7 copy-start.2
  18.0 366.7 %reduce-scatter.2.cloned.1.call-start = ((), (), s32[]{:S(2)}) async-start(), calls=%async_computation.2 | async-start | bytes 4718592 | tf_op jit(solution)/shard_map/reduce_scatter | solution.py:99
  18.1 27.9 %copy-start.5 = (s32[1,16,2]{1,2,0:T(2,128)S(1)}, s32[1,16,2]{1,2,0:T(2,128)}, u32[]{:S(2)}) copy-start(s32[1,16,2]{1,2,0:T(2,128)} %param.23) | copy-start | bytes 388
  18.1 28.8 %copy-start.3 = (s32[640]{0:T(1024)S(1)}, s32[640]{0:T(1024)}, u32[]{:S(2)}) copy-start(s32[640]{0:T(1024)} %param.20) | copy-start | bytes 7684
  324.8 61.0 %copy-start.6 = (bf16[512,256]{1,0:T(8,128)(2,1)S(1)}, bf16[512,256]{1,0:T(8,128)(2,1)}, u32[]{:S(2)}) copy-start(bf16[512,256]{1,0:T(8,128)(2,1)} %param.13) | copy-start | bytes 786436
  324.8 61.0 %copy-start.7 = (bf16[256,256]{1,0:T(8,128)(2,1)S(1)}, bf16[256,256]{1,0:T(8,128)(2,1)}, u32[]{:S(2)}) copy-start(bf16[256,256]{1,0:T(8,128)(2,1)} %param.17) | copy-start | bytes 393220
  332.8 201.6 %all-reduce.3.cloned.1.call-start = ((), (), s32[]{:S(2)}) async-start(), calls=%async_computation.3 | async-start | bytes 1048576 | tf_op jit(solution)/shard_map/psum | solution.py:109
Sparse Core Ops, SparseCore 0:
  18.2 59.5 all-gather.1
  332.9 51.7 reduce-scatter.1
  390.2 144.0 all-reduce.2
where the time goes:
time: 546 us; the launch traced here: 544 us
  waiting for transfers between devices  228 us (42%)
  matrix products  198 us (36%)
  local copies, waits for them, and re-layouts  95.4 us (17%)
  between operations  14.6 us (3%)
  other arithmetic  7.94 us (1%)
    psum x1, waiting for transfers between devices, on_device(): grad_first = lax.psum(grad_first, ('row', 'col'))  146 us
    dot_general x5, matrix products, add_block(): jnp.einsum('kc,kuf->cuf', selector, contrib, precision=lax.Precision.HIGH...  130 us
    dot_general x5, matrix products, add_block(): jnp.einsum('ktu,ktf->kuf', tile_part, gathered_rows, preferred_element_ty...  64.1 us
    reduce_scatter x1, waiting for transfers between devices, on_device(): lax.psum_scatter(summed_tiles.reshape(col_count * tile_size, features), '...  50.9 us
    gather x5, local copies, waits for them, and re-layouts, add_block(): gathered_rows = buffer_tiles[row_part]  43.7 us
    unnamed x23, local copies, waits for them, and re-layouts  39.7 us
    all_gather x1, waiting for transfers between devices, on_device(): gathered = lax.all_gather(message, 'col', axis=0, tiled=True)  30.8 us
  transfers between devices with their start and end apart: 3, of which 3 were waited for; matrix products, arithmetic and copies ran while one was open for 6% of the time, Pallas kernels for 0%

commit v1 on v0

--- a/solution.py
+++ b/solution.py
@@ -106,7 +106,7 @@
     pre_one = jnp.dot(feats_one, weight_one, preferred_element_type=jnp.float32)
     dpre_one = (grad_hidden.astype(jnp.float32) * silu_slope(pre_one)).astype(jnp.bfloat16)
     grad_first = column_product(feats_one, dpre_one)
-    grad_first = lax.psum(grad_first, ("row", "col"))
+    grad_first = jnp.sum(lax.all_gather(grad_first, ("row", "col")), axis=0)
     return (grad_hidden, grad_first * weight_norm, grad_second * weight_norm)
 
 

time: 546 us -> 766 us (1.40)
  waiting for transfers between devices: 228 us -> 425 us
  local copies, waits for them, and re-layouts: 95.4 us -> 125 us
  matrix products: 198 us -> 186 us
    all_gather x0 -> x1, waiting for transfers between devices: none -> 235 us  [on_device(): grad_first = jnp.sum(lax.all_gather(grad_first, ('row', 'col')), axis=0)]
    psum x1, waiting for transfers between devices: 146 us -> 108 us  [on_device(): grad_second = lax.psum(grad_second, ('row', 'col'))]
    unnamed x23 -> x22, local copies, waits for them, and re-layouts: 39.7 us -> 59.2 us
    dot_general x5, matrix products: 130 us -> 117 us  [add_block(): jnp.einsum('kc,kuf->cuf', selector, contrib, precision=lax.Precision.HIGH...]
    while x0 -> x20, local copies, waits for them, and re-layouts: none -> 10.2 us
  transfers between devices with their start and end apart: 3 -> 4, of which waited for: 3 -> 4; matrix products, arithmetic and copies ran while one was open for 6% -> 4% of each run, Pallas kernels for 0% -> 0%
where the time goes in v1:
time: 766 us; the launch traced here: 765 us
  waiting for transfers between devices  425 us (55%)
  matrix products  186 us (24%)
  local copies, waits for them, and re-layouts  125 us (16%)
  between operations  16.4 us (2%)
  other arithmetic  11.1 us (1%)
    all_gather x1, waiting for transfers between devices, on_device(): grad_first = jnp.sum(lax.all_gather(grad_first, ('row', 'col')), axis=0)  235 us
    dot_general x5, matrix products, add_block(): jnp.einsum('kc,kuf->cuf', selector, contrib, precision=lax.Precision.HIGH...  117 us
    psum x1, waiting for transfers between devices, on_device(): grad_second = lax.psum(grad_second, ('row', 'col'))  108 us
    dot_general x5, matrix products, add_block(): jnp.einsum('ktu,ktf->kuf', tile_part, gathered_rows, preferred_element_ty...  64.8 us
    unnamed x22, local copies, waits for them, and re-layouts  59.2 us
    reduce_scatter x1, waiting for transfers between devices, on_device(): lax.psum_scatter(summed_tiles.reshape(col_count * tile_size, features), '...  50.9 us
    gather x5, local copies, waits for them, and re-layouts, add_block(): gathered_rows = buffer_tiles[row_part]  43.7 us
    all_gather x1, waiting for transfers between devices, on_device(): gathered = lax.all_gather(message, 'col', axis=0, tiled=True)  30.7 us
  transfers between devices with their start and end apart: 4, of which 4 were waited for; matrix products, arithmetic and copies ran while one was open for 4% of the time, Pallas kernels for 0%

profile of v1, /device:TPU:1, one launch (start us, length us, event | category | flops | bytes accessed | tf_op | source)
XLA Modules:
  0.0 764.6 jit_solution(1704725487157319184)
XLA Ops:
  11.4 1.6 gather_fusion.1
  13.9 3.5 scatter_fusion
  20.0 27.9 %copy.40 = bf16[640,128,128]{1,2,0:T(8,128)(2,1)} copy(bf16[640,128,128]{2,1,0:T(8,128)(2,1)} %param.19) | data formatting | bytes 41943040 | tf_op args[6]
  48.0 30.7 %all-gather.4.cloned.1.call-done = bf16[8192,256]{1,0:T(8,128)(2,1)} async-done(((bf16[512,256]{1,0:T(8,128)(2,1)}), bf16[8192,256]{1,0:T(8,128)(2,1)}) %all-gather.4.cloned.1.call-update) | async-done | bytes 4194320 | tf_op jit(solution)/shard_map/all_gather | solution.py:59
  78.7 239.5 %while.11 = (s32[]{:T(128)}, f32[32,128,256]{2,0,1:T(8,128)}, s32[5,128]{1,0:T(8,128)}, f32[5,128]{1,0:T(8,128)S(1)}, bf16[5,128,128,128]{2,3,1,0:T(8,128)(2,1)}...) while((s32[]{:T(128)}, f32[32,128,256]{2,0,1:T(8,128)}, ...), condition=%wide.region_5.6_spmd.clone, body=%wide.region_4.5_spmd.clone.sunk | while | flops 2686461440 | bytes 104867000 | solution.py:89
  79.4 8.7 %gather_fusion = bf16[128,128,256]{2,1,0:T(8,128)(2,1)} fusion(bf16[64,128,256]{2,1,0:T(8,128)(2,1)} %get-tuple-element.170, s32[1024]{0:T(1024)S(1)} %pad_clamp_fusion.3), kind=kCustom, calls=%fused_computation.clone.clone.1 | custom fusion | bytes 16777728 | tf_op jit(solution)/shard_map/while/body/eval_jaxpr/gather | solution.py:74
  88.1 13.0 %fusion.55 = f32[128,128,256]{2,1,0:T(8,128)} fusion(bf16[128,128,256]{2,1,0:T(8,128)(2,1)} %gather_fusion, bf16[5,128,128,128]{2,3,1,0:T(8,128)(2,1)} %get-tuple-element.168, s32[]{:T(128)S(6)} %copy.69), kind=kOutput, calls=%fused_computation.6.clone.1 | convolution fusion | flops 1073741824 | bytes 29360132 | tf_op jit(solution)/shard_map/while/body/eval_jaxpr/ktu,ktf->kuf/dot_general | solution.py:75
  101.1 23.4 %select_add_fusion.2 = f32[32,128,256]{2,0,1:T(8,128)S(1)} fusion(f32[32,128,256]{2,0,1:T(8,128)S(1)} %copy-done.1, pred[]{:T(512)S(6)} %compare.5, f32[128,128,256]{2,1,0:T(8,128)} %fusion.55, f32[128]{0:T(128)S(1)} %fusion.56, s32[128]{0:T(128)S(1)} %fusion.57), kind=kOutput, calls=%fused_computation.8.clone.1 | convolution fusion | flops 1612718080 | bytes 25166848 | tf_op jit(solution)/shard_map/while/body/eval_jaxpr/kc,kuf->cuf/dot_general | solution.py:79
  124.5 2.0 copy-done.2
  127.3 8.7 %gather_fusion = bf16[128,128,256]{2,1,0:T(8,128)(2,1)} fusion(bf16[64,128,256]{2,1,0:T(8,128)(2,1)} %get-tuple-element.170, s32[1024]{0:T(1024)S(1)} %pad_clamp_fusion.3), kind=kCustom, calls=%fused_computation.clone.clone.1 | custom fusion | bytes 16777728 | tf_op jit(solution)/shard_map/while/body/eval_jaxpr/gather | solution.py:74
  136.0 13.0 %fusion.55 = f32[128,128,256]{2,1,0:T(8,128)} fusion(bf16[128,128,256]{2,1,0:T(8,128)(2,1)} %gather_fusion, bf16[5,128,128,128]{2,3,1,0:T(8,128)(2,1)} %get-tuple-element.168, s32[]{:T(128)S(6)} %copy.69), kind=kOutput, calls=%fused_computation.6.clone.1 | convolution fusion | flops 1073741824 | bytes 29360132 | tf_op jit(solution)/shard_map/while/body/eval_jaxpr/ktu,ktf->kuf/dot_general | solution.py:75
  149.0 23.4 %select_add_fusion.2 = f32[32,128,256]{2,0,1:T(8,128)S(1)} fusion(f32[32,128,256]{2,0,1:T(8,128)S(1)} %copy-done.1, pred[]{:T(512)S(6)} %compare.5, f32[128,128,256]{2,1,0:T(8,128)} %fusion.55, f32[128]{0:T(128)S(1)} %fusion.56, s32[128]{0:T(128)S(1)} %fusion.57), kind=kOutput, calls=%fused_computation.8.clone.1 | convolution fusion | flops 1612718080 | bytes 25166848 | tf_op jit(solution)/shard_map/while/body/eval_jaxpr/kc,kuf->cuf/dot_general | solution.py:79
  172.4 2.0 copy-done.2
  175.2 8.7 %gather_fusion = bf16[128,128,256]{2,1,0:T(8,128)(2,1)} fusion(bf16[64,128,256]{2,1,0:T(8,128)(2,1)} %get-tuple-element.170, s32[1024]{0:T(1024)S(1)} %pad_clamp_fusion.3), kind=kCustom, calls=%fused_computation.clone.clone.1 | custom fusion | bytes 16777728 | tf_op jit(solution)/shard_map/while/body/eval_jaxpr/gather | solution.py:74
  183.9 13.0 %fusion.55 = f32[128,128,256]{2,1,0:T(8,128)} fusion(bf16[128,128,256]{2,1,0:T(8,128)(2,1)} %gather_fusion, bf16[5,128,128,128]{2,3,1,0:T(8,128)(2,1)} %get-tuple-element.168, s32[]{:T(128)S(6)} %copy.69), kind=kOutput, calls=%fused_computation.6.clone.1 | convolution fusion | flops 1073741824 | bytes 29360132 | tf_op jit(solution)/shard_map/while/body/eval_jaxpr/ktu,ktf->kuf/dot_general | solution.py:75
  196.9 23.4 %select_add_fusion.2 = f32[32,128,256]{2,0,1:T(8,128)S(1)} fusion(f32[32,128,256]{2,0,1:T(8,128)S(1)} %copy-done.1, pred[]{:T(512)S(6)} %compare.5, f32[128,128,256]{2,1,0:T(8,128)} %fusion.55, f32[128]{0:T(128)S(1)} %fusion.56, s32[128]{0:T(128)S(1)} %fusion.57), kind=kOutput, calls=%fused_computation.8.clone.1 | convolution fusion | flops 1612718080 | bytes 25166848 | tf_op jit(solution)/shard_map/while/body/eval_jaxpr/kc,kuf->cuf/dot_general | solution.py:79
  220.3 2.0 copy-done.2
  223.1 8.8 %gather_fusion = bf16[128,128,256]{2,1,0:T(8,128)(2,1)} fusion(bf16[64,128,256]{2,1,0:T(8,128)(2,1)} %get-tuple-element.170, s32[1024]{0:T(1024)S(1)} %pad_clamp_fusion.3), kind=kCustom, calls=%fused_computation.clone.clone.1 | custom fusion | bytes 16777728 | tf_op jit(solution)/shard_map/while/body/eval_jaxpr/gather | solution.py:74
  231.8 13.0 %fusion.55 = f32[128,128,256]{2,1,0:T(8,128)} fusion(bf16[128,128,256]{2,1,0:T(8,128)(2,1)} %gather_fusion, bf16[5,128,128,128]{2,3,1,0:T(8,128)(2,1)} %get-tuple-element.168, s32[]{:T(128)S(6)} %copy.69), kind=kOutput, calls=%fused_computation.6.clone.1 | convolution fusion | flops 1073741824 | bytes 29360132 | tf_op jit(solution)/shard_map/while/body/eval_jaxpr/ktu,ktf->kuf/dot_general | solution.py:75
  244.8 23.4 %select_add_fusion.2 = f32[32,128,256]{2,0,1:T(8,128)S(1)} fusion(f32[32,128,256]{2,0,1:T(8,128)S(1)} %copy-done.1, pred[]{:T(512)S(6)} %compare.5, f32[128,128,256]{2,1,0:T(8,128)} %fusion.55, f32[128]{0:T(128)S(1)} %fusion.56, s32[128]{0:T(128)S(1)} %fusion.57), kind=kOutput, calls=%fused_computation.8.clone.1 | convolution fusion | flops 1612718080 | bytes 25166848 | tf_op jit(solution)/shard_map/while/body/eval_jaxpr/kc,kuf->cuf/dot_general | solution.py:79
  268.2 2.0 copy-done.2
  271.0 8.8 %gather_fusion = bf16[128,128,256]{2,1,0:T(8,128)(2,1)} fusion(bf16[64,128,256]{2,1,0:T(8,128)(2,1)} %get-tuple-element.170, s32[1024]{0:T(1024)S(1)} %pad_clamp_fusion.3), kind=kCustom, calls=%fused_computation.clone.clone.1 | custom fusion | bytes 16777728 | tf_op jit(solution)/shard_map/while/body/eval_jaxpr/gather | solution.py:74
  279.7 13.0 %fusion.55 = f32[128,128,256]{2,1,0:T(8,128)} fusion(bf16[128,128,256]{2,1,0:T(8,128)(2,1)} %gather_fusion, bf16[5,128,128,128]{2,3,1,0:T(8,128)(2,1)} %get-tuple-element.168, s32[]{:T(128)S(6)} %copy.69), kind=kOutput, calls=%fused_computation.6.clone.1 | convolution fusion | flops 1073741824 | bytes 29360132 | tf_op jit(solution)/shard_map/while/body/eval_jaxpr/ktu,ktf->kuf/dot_general | solution.py:75
  292.7 23.4 %select_add_fusion.2 = f32[32,128,256]{2,0,1:T(8,128)S(1)} fusion(f32[32,128,256]{2,0,1:T(8,128)S(1)} %copy-done.1, pred[]{:T(512)S(6)} %compare.5, f32[128,128,256]{2,1,0:T(8,128)} %fusion.55, f32[128]{0:T(128)S(1)} %fusion.56, s32[128]{0:T(128)S(1)} %fusion.57), kind=kOutput, calls=%fused_computation.8.clone.1 | convolution fusion | flops 1612718080 | bytes 25166848 | tf_op jit(solution)/shard_map/while/body/eval_jaxpr/kc,kuf->cuf/dot_general | solution.py:79
  316.1 2.0 copy-done.2
  318.2 5.9 copy.49
  324.1 8.0 %copy.63 = f32[32,8,32,128]{3,1,2,0:T(8,128)} copy(f32[32,8,32,128]{3,2,1,0:T(8,128)} %bitcast.68) | data formatting | bytes 8388608
  333.2 50.9 %reduce-scatter.2.cloned.1.call-done = f32[512,256]{0,1:T(8,128)} async-done(((f32[4096,256]{0,1:T(8,128)}), f32[512,256]{0,1:T(8,128)}) %reduce-scatter.2.cloned.1.call-update) | async-done | bytes 524304 | tf_op jit(solution)/shard_map/reduce_scatter | solution.py:99
  386.4 108.4 %all-reduce.2.cloned.1.call-done = f32[256,256]{0,1:T(8,128)} async-done(((f32[256,256]{0,1:T(8,128)}), f32[256,256]{0,1:T(8,128)}) %all-reduce.2.cloned.1.call-update) | async-done | bytes 262160 | tf_op jit(solution)/shard_map/psum | solution.py:55
  497.4 235.2 %all-gather.6.cloned.1.call-done = f32[32768,256]{0,1:T(8,128)} async-done(((f32[256,256]{0,1:T(8,128)}), f32[32768,256]{0,1:T(8,128)}) %all-gather.6.cloned.1.call-update) | async-done | bytes 33554448 | tf_op jit(solution)/shard_map/all_gather | solution.py:109
  732.6 19.6 %copy.57 = f32[32,8,128,256]{3,2,1,0:T(8,128)S(1)} copy(f32[32,8,128,256]{3,1,2,0:T(8,128)} %bitcast.66) | data formatting | bytes 67108864
  752.2 4.1 bitcast_reduce_fusion
  (85 shorter events, 16.6 us)
Async XLA Ops:
  8.0 1.9 copy-start
  8.0 5.9 copy-start.5
  8.0 70.6 %all-gather.4.cloned.1.call-start = ((), (), s32[]{:S(2)}) async-start(), calls=%async_computation.1 | async-start | bytes 4456448 | tf_op jit(solution)/shard_map/all_gather | solution.py:59
  13.1 4.7 copy-start.3
  13.3 6.5 copy-start.6
  18.9 365.2 %reduce-scatter.2.cloned.1.call-start = ((), (), s32[]{:S(2)}) async-start(), calls=%async_computation.2 | async-start | bytes 4718592 | tf_op jit(solution)/shard_map/reduce_scatter | solution.py:99
  20.0 27.9 %copy-start.4 = (s32[640]{0:T(1024)S(1)}, s32[640]{0:T(1024)}, u32[]{:S(2)}) copy-start(s32[640]{0:T(1024)} %param.20) | copy-start | bytes 7684
  88.1 13.0 %copy-start.1 = (f32[32,128,256]{2,0,1:T(8,128)S(1)}, f32[32,128,256]{2,0,1:T(8,128)}, u32[]{:S(2)}) copy-start(f32[32,128,256]{2,0,1:T(8,128)} %get-tuple-element.156) | copy-start | bytes 12582916 | tf_op jit(solution)/shard_map/while
  124.5 2.0 copy-start.2
  136.0 13.0 %copy-start.1 = (f32[32,128,256]{2,0,1:T(8,128)S(1)}, f32[32,128,256]{2,0,1:T(8,128)}, u32[]{:S(2)}) copy-start(f32[32,128,256]{2,0,1:T(8,128)} %get-tuple-element.156) | copy-start | bytes 12582916 | tf_op jit(solution)/shard_map/while
  172.4 2.0 copy-start.2
  183.9 13.0 %copy-start.1 = (f32[32,128,256]{2,0,1:T(8,128)S(1)}, f32[32,128,256]{2,0,1:T(8,128)}, u32[]{:S(2)}) copy-start(f32[32,128,256]{2,0,1:T(8,128)} %get-tuple-element.156) | copy-start | bytes 12582916 | tf_op jit(solution)/shard_map/while
  220.3 2.0 copy-start.2
  231.8 13.0 %copy-start.1 = (f32[32,128,256]{2,0,1:T(8,128)S(1)}, f32[32,128,256]{2,0,1:T(8,128)}, u32[]{:S(2)}) copy-start(f32[32,128,256]{2,0,1:T(8,128)} %get-tuple-element.156) | copy-start | bytes 12582916 | tf_op jit(solution)/shard_map/while
  268.2 2.0 copy-start.2
  279.7 13.0 %copy-start.1 = (f32[32,128,256]{2,0,1:T(8,128)S(1)}, f32[32,128,256]{2,0,1:T(8,128)}, u32[]{:S(2)}) copy-start(f32[32,128,256]{2,0,1:T(8,128)} %get-tuple-element.156) | copy-start | bytes 12582916 | tf_op jit(solution)/shard_map/while
  316.1 2.0 copy-start.2
  324.1 61.0 %copy-start.7 = (bf16[512,256]{1,0:T(8,128)(2,1)S(1)}, bf16[512,256]{1,0:T(8,128)(2,1)}, u32[]{:S(2)}) copy-start(bf16[512,256]{1,0:T(8,128)(2,1)} %param.13) | copy-start | bytes 786436
  324.1 61.0 %copy-start.8 = (bf16[256,256]{1,0:T(8,128)(2,1)S(1)}, bf16[256,256]{1,0:T(8,128)(2,1)}, u32[]{:S(2)}) copy-start(bf16[256,256]{1,0:T(8,128)(2,1)} %param.17) | copy-start | bytes 393220
  332.1 162.7 %all-reduce.2.cloned.1.call-start = ((), (), s32[]{:S(2)}) async-start(), calls=%async_computation.3 | async-start | bytes 524288 | tf_op jit(solution)/shard_map/psum | solution.py:55
  333.1 399.5 %all-gather.6.cloned.1.call-start = ((), (), s32[]{:S(2)}) async-start(), calls=%async_computation.4 | async-start | bytes 33816576 | tf_op jit(solution)/shard_map/all_gather | solution.py:109
Sparse Core Ops, SparseCore 0:
  19.0 59.5 all-gather.3
  332.2 51.7 reduce-scatter.1
Sparse Core Ops, SparseCore 1:
  337.9 156.8 all-reduce.1
  497.0 235.6 all-gather.5
